TPU v7x, 256 devices: a whole 4x4x8 slice. The times are simulated.
256 devices in a mesh: lat: 16 (over y, x), kpt: 16 (over z, core).
Axes of the slice: x: 4, y: 4, z: 8, core: 2. Of those that a mesh axis runs over, the one named last changes fastest.
Arguments:
- coarse: bfloat16 [2, 16, 256, 12288], P(None, 'lat', 'kpt'), may hold values from -0.1875 to 0.1875
- rp_vectors: int32 [16, 3], P('lat'), may hold values from -4 to 4
- rp_weights: int32 [16], P('lat'), may hold values from 1 to 3
- re_vectors: int32 [256, 3], replicated, may hold values from -4 to 4
- re_weights: int32 [256], replicated, may hold values from 1 to 3
- q_points: float32 [2, 3], replicated, may hold values from 0 to 1
- k_points: float32 [1024, 3], P('kpt'), may hold values from 0 to 1
- modes_rot: bfloat16 [2, 2, 48, 48], replicated, may hold values from -0.625 to 0.625
- u_k: bfloat16 [2, 1024, 16, 16], P(None, 'kpt'), may hold values from -1 to 1
- u_kq: bfloat16 [2, 2, 1024, 16, 16], P(None, None, 'kpt'), may hold values from -1 to 1
- mask_k: int32 [1024, 16], P('kpt'), may hold values 0 or 1
- mask_kq: int32 [2, 1024, 16], P(None, 'kpt'), may hold values 0 or 1
Outputs:
- coupling: bfloat16 [2, 1024, 2, 12288], P(None, 'kpt', None, 'lat')
All inputs are finite; a program needn't handle non-finite values. No bound on the sum of `mask_k` or of `mask_kq` on one device may be relied on, other than what follows from the above.
Results may differ from a plain program's by a relative error of at most 0.017.
Values may be sent and summed in bfloat16 or wider, within the bound.
No kernel may reach another device: no remote copies, remote signals or barrier semaphores. Data moves between devices by JAX's collectives and lax.ppermute only.
A program may use at most 64 MiB of HBM per device.

v0:
```python
import jax
import jax.numpy as jnp
from jax import lax
from jax.sharding import PartitionSpec as P

two_pi = 6.283185307179586


def phases(points, vectors, weights):
    cells = vectors.astype(jnp.float32)
    argument = two_pi * (
        points[:, 0:1] * cells[None, :, 0]
        + points[:, 1:2] * cells[None, :, 1]
        + points[:, 2:3] * cells[None, :, 2]
    )
    inverse = 1.0 / weights.astype(jnp.float32)
    return (
        (jnp.cos(argument) * inverse).astype(jnp.bfloat16),
        (jnp.sin(argument) * inverse).astype(jnp.bfloat16),
    )


def rotate_modes(values, modes_rot):
    shape = values.shape
    mode_count = modes_rot.shape[2]
    split = values.reshape(shape[0], shape[1], shape[2], mode_count, shape[3] // mode_count)
    br = jnp.einsum(
        "qmn,qrmx->qrnx", modes_rot[0], split[0], preferred_element_type=jnp.float32
    ) - jnp.einsum("qmn,qrmx->qrnx", modes_rot[1], split[1], preferred_element_type=jnp.float32)
    bi = jnp.einsum(
        "qmn,qrmx->qrnx", modes_rot[0], split[1], preferred_element_type=jnp.float32
    ) + jnp.einsum("qmn,qrmx->qrnx", modes_rot[1], split[0], preferred_element_type=jnp.float32)
    return jnp.stack([br, bi]).reshape(shape).astype(jnp.bfloat16)


def phonon_sum(block, vectors, weights, q_points):
    phase_real, phase_imag = phases(q_points, vectors, weights)
    rows = block.shape[1]
    cells = block.shape[2]
    lanes = block.shape[3]
    flat_real = block[0].reshape(rows, cells * lanes)
    flat_imag = block[1].reshape(rows, cells * lanes)
    part_real = jnp.dot(phase_real, flat_real, preferred_element_type=jnp.float32) - jnp.dot(
        phase_imag, flat_imag, preferred_element_type=jnp.float32
    )
    part_imag = jnp.dot(phase_real, flat_imag, preferred_element_type=jnp.float32) + jnp.dot(
        phase_imag, flat_real, preferred_element_type=jnp.float32
    )
    return jnp.stack([part_real, part_imag]).reshape(2, q_points.shape[0], cells, lanes)


def per_device(
    coarse,
    rp_vectors,
    rp_weights,
    re_vectors,
    re_weights,
    q_points,
    k_points,
    modes_rot,
    u_k,
    u_kq,
    mask_k,
    mask_kq,
):
    q_count = q_points.shape[0]
    k_count = k_points.shape[0]
    band_count = u_k.shape[2]
    partial_value = phonon_sum(coarse, rp_vectors, rp_weights, q_points)
    summed = lax.psum_scatter(partial_value, "lat", scatter_dimension=2, tiled=True).astype(
        jnp.bfloat16
    )
    rotated = rotate_modes(summed, modes_rot)
    shared = lax.all_to_all(rotated, "lat", split_axis=3, concat_axis=2, tiled=True)
    lane_local = shared.shape[3]
    portion = lax.all_gather(shared, "kpt", axis=2, tiled=True)
    kreal, kimag = phases(k_points, re_vectors, re_weights)
    er = jnp.einsum(
        "kr,qrx->kqx", kreal, portion[0], preferred_element_type=jnp.float32
    ) - jnp.einsum("kr,qrx->kqx", kimag, portion[1], preferred_element_type=jnp.float32)
    ei = jnp.einsum(
        "kr,qrx->kqx", kreal, portion[1], preferred_element_type=jnp.float32
    ) + jnp.einsum("kr,qrx->kqx", kimag, portion[0], preferred_element_type=jnp.float32)
    totals = jnp.stack([er, ei])
    mode_local = lane_local // (band_count * band_count)
    field = totals.astype(jnp.bfloat16).reshape(
        2, k_count, q_count, mode_local, band_count, band_count
    )
    tr = jnp.einsum(
        "kqmab,kbn->kqman", field[0], u_k[0], preferred_element_type=jnp.float32
    ) - jnp.einsum("kqmab,kbn->kqman", field[1], u_k[1], preferred_element_type=jnp.float32)
    ti = jnp.einsum(
        "kqmab,kbn->kqman", field[0], u_k[1], preferred_element_type=jnp.float32
    ) + jnp.einsum("kqmab,kbn->kqman", field[1], u_k[0], preferred_element_type=jnp.float32)
    tr = tr.astype(jnp.bfloat16)
    ti = ti.astype(jnp.bfloat16)
    outr = jnp.einsum(
        "qkac,kqman->kqmcn", u_kq[0], tr, preferred_element_type=jnp.float32
    ) + jnp.einsum("qkac,kqman->kqmcn", u_kq[1], ti, preferred_element_type=jnp.float32)
    outi = jnp.einsum(
        "qkac,kqman->kqmcn", u_kq[0], ti, preferred_element_type=jnp.float32
    ) - jnp.einsum("qkac,kqman->kqmcn", u_kq[1], tr, preferred_element_type=jnp.float32)
    window = (
        jnp.transpose(mask_kq.astype(jnp.float32), (1, 0, 2))[:, :, None, :, None]
        * mask_k.astype(jnp.float32)[:, None, None, None, :]
    )
    result = jnp.stack([outr * window, outi * window])
    return result.reshape(2, k_count, q_count, lane_local).astype(jnp.bfloat16)


def solution(mesh):
    placed = (
        P(None, "lat", "kpt", None),
        P("lat", None),
        P("lat"),
        P(),
        P(),
        P(),
        P("kpt", None),
        P(),
        P(None, "kpt", None, None),
        P(None, None, "kpt", None, None),
        P("kpt", None),
        P(None, "kpt", None),
    )
    return jax.shard_map(
        per_device,
        mesh=mesh,
        in_specs=placed,
        out_specs=P(None, "kpt", None, "lat"),
        check_vma=False,
    )
```

profile of v0, /device:TPU:1, one launch (start us, length us, event | category | flops | bytes accessed | tf_op | source)
XLA Modules:
  0.0 256.3 jit_solution(5092199044945277099)
XLA Ops:
  7.2 0.7 convert_element_type.53
  8.5 1.2 convert_bitcast_fusion.1
  10.4 2.1 convert_reduce_fusion.1
  12.4 1.5 multiply_subtract_fusion
  13.9 1.4 pad_maximum_fusion
  15.4 86.5 %all-reduce.2 = bf16[2,2,16,12288]{3,1,2,0:T(2,128)(2,1)} all-reduce(f32[2,2,16,12288]{3,1,2,0:T(2,128)S(1)} %pad_maximum_fusion), channel_id=2, replica_groups=mesh['lat'=16,'kpt'=16] {'lat'}, use_global_device_ids=true, to_apply=%region_0.0.clone | all-reduce | flops 786432 | bytes 4718592
  102.5 1.6 dynamic-slice_convert_fusion
  105.1 10.0 %copy.99 = bf16[2,2,1,12288]{1,0,2,3:T(2,128)(2,1)} copy(bf16[2,2,1,12288]{3,1,2,0:T(2,128)(2,1)S(1)} %pad_maximum_fusion.2) | data formatting | bytes 196608 | tf_op jit(solution)/shard_map/stack | solution.py:33
  115.1 13.7 %reshape.158 = bf16[16,2,1536]{2,1,0:T(2,128)(2,1)S(1)} reshape(bf16[12288,1,2,2]{3,2,1,0:T(2,128)(2,1)} %bitcast.147) | data formatting | bytes 196608
  128.8 9.2 %all_to_all.12 = bf16[16,2,1536]{2,1,0:T(2,128)(2,1)S(1)} all-to-all(bf16[16,2,1536]{2,1,0:T(2,128)(2,1)S(1)} %reshape.158), channel_id=1, replica_groups=mesh['lat'=16,'kpt'=16] {'lat'}, dimensions={0} | all-to-all | bytes 196608 | tf_op jit(solution)/shard_map/all_to_all | solution.py:74
  138.0 14.7 %reshape.159 = bf16[12288,1,2,2]{3,2,1,0:T(2,128)(2,1)} reshape(bf16[16,2,1536]{2,1,0:T(2,128)(2,1)S(1)} %all_to_all.12) | data formatting | bytes 196608
  152.8 9.9 %copy.128 = bf16[2,2,16,768]{3,2,1,0:T(8,128)(2,1)} copy(bf16[2,2,16,768]{1,0,3,2:T(2,128)(2,1)} %bitcast.148) | data formatting | bytes 196608 | tf_op jit(solution)/shard_map/all_to_all | solution.py:74
  163.0 1.0 copy.134
  164.0 1.5 copy.136
  165.5 1.5 copy.135
  167.1 0.7 broadcast_multiply_fusion
  167.8 45.9 %all-gather.2.cloned.1.call-done = bf16[2,2,256,768]{3,2,1,0:T(8,128)(2,1)} async-done(((bf16[2,2,16,768]{3,2,1,0:T(8,128)(2,1)}), bf16[2,2,256,768]{3,2,1,0:T(8,128)(2,1)}) %all-gather.2.cloned.1.call-update) | async-done | bytes 1572880 | tf_op jit(solution)/shard_map/all_gather | solution.py:76
  213.8 1.7 fusion.9
  215.5 1.6 fusion.1
  217.1 0.9 copy.104
  219.3 1.3 copy.103
  220.6 2.2 copy.106
  222.8 1.5 fusion.21
  226.8 2.4 fusion.10
  229.8 2.3 fusion.14
  232.1 2.3 fusion.12
  234.4 3.4 %copy.118 = f32[64,2,3,16,16]{0,3,4,2,1:T(8,128)} copy(f32[64,2,3,16,16]{4,3,2,1,0:T(8,128)} %fusion.10) | data formatting | bytes 786432 | tf_op jit(solution)/shard_map/qkac,kqman->kqmcn/dot_general | solution.py:102
  237.9 2.3 copy.113
  240.1 3.6 %copy.117 = f32[64,2,3,16,16]{0,3,4,2,1:T(8,128)} copy(f32[64,2,3,16,16]{4,3,2,1,0:T(8,128)} %fusion.14) | data formatting | bytes 786432 | tf_op jit(solution)/shard_map/qkac,kqman->kqmcn/dot_general | solution.py:100
  243.8 2.3 copy.114
  246.1 2.1 fusion.7
  248.3 1.1 copy.119
  (63 shorter events, 7.7 us)
Async XLA Ops:
  6.5 207.2 %all-gather.2.cloned.1.call-start = ((), (), s32[]{:S(2)}) async-start(), calls=%async_computation.1 | async-start | bytes 1671168 | tf_op jit(solution)/shard_map/all_gather | solution.py:76
  9.7 0.7 copy-start.10
  15.3 86.6 %copy-start.15 = (u32[256]{0:T(256)S(1)}, u32[256]{0:T(256)}, u32[]{:S(2)}) copy-start(u32[256]{0:T(256)} %constant.12) | copy-start | bytes 3076
  15.4 88.8 %copy-start.7 = (bf16[2,2,48,48]{3,2,1,0:T(8,128)(2,1)S(1)}, bf16[2,2,48,48]{3,2,1,0:T(8,128)(2,1)}, u32[]{:S(2)}) copy-start(bf16[2,2,48,48]{3,2,1,0:T(8,128)(2,1)} %param.19) | copy-start | bytes 55300
  152.7 9.9 %copy-start.12 = (s32[256,3]{0,1:T(4,128)S(1)}, s32[256,3]{0,1:T(4,128)}, u32[]{:S(2)}) copy-start(s32[256,3]{0,1:T(4,128)} %param.15) | copy-start | bytes 9220
  152.7 10.0 %copy-start.11 = (s32[64,16]{0,1:T(8,128)S(1)}, s32[64,16]{0,1:T(8,128)}, u32[]{:S(2)}) copy-start(s32[64,16]{0,1:T(8,128)} %param.22) | copy-start | bytes 12292
  152.8 10.0 %copy-start.8 = (bf16[2,64,16,16]{1,3,2,0:T(8,128)(2,1)S(1)}, bf16[2,64,16,16]{1,3,2,0:T(8,128)(2,1)}, u32[]{:S(2)}) copy-start(bf16[2,64,16,16]{1,3,2,0:T(8,128)(2,1)} %param.20) | copy-start | bytes 196612
  152.8 11.2 %copy-start.6 = (bf16[2,2,64,16,16]{2,4,3,1,0:T(8,128)(2,1)S(1)}, bf16[2,2,64,16,16]{2,4,3,1,0:T(8,128)(2,1)}, u32[]{:S(2)}) copy-start(bf16[2,2,64,16,16]{2,4,3,1,0:T(8,128)(2,1)} %param.21) | copy-start | bytes 393220
  162.6 4.4 %copy-start.14 = (s32[256]{0:T(256)S(1)}, s32[256]{0:T(256)}, u32[]{:S(2)}) copy-start(s32[256]{0:T(256)} %param.16) | copy-start | bytes 3076
  162.7 4.4 %copy-start.13 = (f32[64,3]{0,1:T(4,128)S(1)}, f32[64,3]{0,1:T(4,128)}, u32[]{:S(2)}) copy-start(f32[64,3]{0,1:T(4,128)} %param.18) | copy-start | bytes 2308
  162.7 4.5 %copy-start.9 = (s32[2,64,16]{1,2,0:T(8,128)S(1)}, s32[2,64,16]{1,2,0:T(8,128)}, u32[]{:S(2)}) copy-start(s32[2,64,16]{1,2,0:T(8,128)} %param.23) | copy-start | bytes 24580
  213.7 4.3 %copy-start.1 = (bf16[2,2,256,768]{3,2,1,0:T(8,128)(2,1)S(1)}, bf16[2,2,256,768]{3,2,1,0:T(8,128)(2,1)}, u32[]{:S(2)}) copy-start(bf16[2,2,256,768]{3,2,1,0:T(8,128)(2,1)} %all-gather.2.cloned.1.call-done) | copy-start | bytes 4718596
  224.8 1.0 copy-start.4
  225.8 1.0 copy-start.2
  226.8 2.4 copy-start.3
  240.1 3.6 %copy-start = (f32[64,2,3,16,16]{4,3,2,1,0:T(8,128)S(1)}, f32[64,2,3,16,16]{4,3,2,1,0:T(8,128)}, u32[]{:S(2)}) copy-start(f32[64,2,3,16,16]{4,3,2,1,0:T(8,128)} %fusion.12) | copy-start | bytes 1179652
  243.8 2.3 copy-start.5
Sparse Core Ops, SparseCore 0:
  162.8 50.9 all-gather.1
where the time goes:
time: 257 us; the launch traced here: 256 us
  blocking collectives  95.8 us (37%)
  local copies, waits for them, and re-layouts  74.4 us (29%)
  waiting for transfers between devices  45.9 us (18%)
  matrix products  15.8 us (6%)
  between operations  14.4 us (6%)
  other arithmetic  9.95 us (4%)
    unnamed x1, blocking collectives  86.5 us
    all_gather x1, waiting for transfers between devices, per_device(): portion = lax.all_gather(shared, 'kpt', axis=2, tiled=True)  45.9 us
    unnamed x41, local copies, waits for them, and re-layouts  34.8 us
    another operation x3, local copies, waits for them, and re-layouts, rotate_modes(): return jnp.stack([br, bi]).reshape(shape).astype(jnp.bfloat16)  10 us
    all_to_all x1, local copies, waits for them, and re-layouts, per_device(): lax.all_to_all(rotated, 'lat', split_axis=3, concat_axis=2, tiled=True)  9.89 us
    all_to_all x1, blocking collectives, per_device(): lax.all_to_all(rotated, 'lat', split_axis=3, concat_axis=2, tiled=True)  9.25 us
  transfers between devices with their start and end apart: 1, of which 1 were waited for; matrix products, arithmetic and copies ran while one was open for 2% of the time, Pallas kernels for 0%

commit v1 on v0

--- a/solution.py
+++ b/solution.py
@@ -1,9 +1,39 @@
+import functools
 import jax
 import jax.numpy as jnp
 from jax import lax
 from jax.sharding import PartitionSpec as P
+from jax.lax import axis_index, axis_size, ppermute
 
 two_pi = 6.283185307179586
+
+
+def pack_quarters(obj, row_dim, load):
+    u1, then = (obj.shape[:row_dim], obj.shape[row_dim + 1 :])
+    u_next = obj.reshape(*u1, load, -1, *then)
+    return jnp.moveaxis(u_next, row_dim, 0)
+
+
+def refer_samples_all(array_here, d_out):
+    array_here = jnp.moveaxis(array_here, 0, d_out)
+    s_next = array_here.shape
+    return array_here.reshape(
+        *s_next[:d_out], s_next[d_out] * s_next[d_out + 1], *s_next[d_out + 2 :]
+    )
+
+
+def prepare_orders(mine_x, shard_axis, mine, mat):
+    y1, small = (axis_size(shard_axis), axis_index(shard_axis))
+    mixed_arr = pack_quarters(mine_x, mine, y1)
+    made = [mixed_arr[small]]
+    for h in range(1, y1):
+        arr_next = mixed_arr[small ^ h]
+        made.append(ppermute(arr_next, shard_axis, [(d, d ^ h) for d in range(y1)]))
+    mixed_arr = jnp.stack(made)[small ^ jnp.arange(y1)]
+    return refer_samples_all(mixed_arr, mat)
+
+
+unite_levels_all = functools.partial(prepare_orders, shard_axis="lat", mine=3, mat=2)
 
 
 def phases(points, vectors, weights):
@@ -71,7 +101,7 @@
         jnp.bfloat16
     )
     rotated = rotate_modes(summed, modes_rot)
-    shared = lax.all_to_all(rotated, "lat", split_axis=3, concat_axis=2, tiled=True)
+    shared = unite_levels_all(rotated)
     lane_local = shared.shape[3]
     portion = lax.all_gather(shared, "kpt", axis=2, tiled=True)
     kreal, kimag = phases(k_points, re_vectors, re_weights)

time: 257 us -> 268 us (1.043)
  waiting for transfers between devices: 45.9 us -> 104 us
  local copies, waits for them, and re-layouts: 74.4 us -> 28.3 us
  blocking collectives: 95.8 us -> 86.6 us
  starting transfers between devices: 0.01 us -> 8.94 us
    ppermute x0 -> x15, waiting for transfers between devices: none -> 45.9 us  [prepare_orders(): made.append(ppermute(arr_next, shard_axis, [(d, d ^ h) for d in range(y1)]))]
    unnamed x41 -> x55, local copies, waits for them, and re-layouts: 34.8 us -> 6.61 us
    all_gather x1, waiting for transfers between devices: 45.9 us -> 57.7 us  [per_device(): portion = lax.all_gather(shared, 'kpt', axis=2, tiled=True)]
    all_to_all x1 -> x0, local copies, waits for them, and re-layouts: 9.89 us -> none  [per_device(): lax.all_to_all(rotated, 'lat', split_axis=3, concat_axis=2, tiled=True)]
    another operation x3, local copies, waits for them, and re-layouts: 10 us -> 0.11 us  [rotate_modes(): return jnp.stack([br, bi]).reshape(shape).astype(jnp.bfloat16)]
    all_to_all x1 -> x0, blocking collectives: 9.25 us -> none  [per_device(): lax.all_to_all(rotated, 'lat', split_axis=3, concat_axis=2, tiled=True)]
    ppermute x0 -> x15, starting transfers between devices: none -> 8.94 us  [prepare_orders(): made.append(ppermute(arr_next, shard_axis, [(d, d ^ h) for d in range(y1)]))]
  transfers between devices with their start and end apart: 1 -> 16, of which waited for: 1 -> 12; matrix products, arithmetic and copies ran while one was open for 2% -> 2% of each run, Pallas kernels for 0% -> 0%
where the time goes in v1:
time: 268 us
  waiting for transfers between devices  104 us (39%)
  blocking collectives  86.6 us (32%)
  local copies, waits for them, and re-layouts  28.3 us (11%)
  matrix products  15.8 us (6%)
  between operations  14.6 us (5%)
  other arithmetic  9.93 us (4%)
  starting transfers between devices  8.94 us (3%)
    unnamed x1, blocking collectives  86.6 us
    all_gather x1, waiting for transfers between devices, per_device(): portion = lax.all_gather(shared, 'kpt', axis=2, tiled=True)  57.7 us
    ppermute x15, waiting for transfers between devices, prepare_orders(): made.append(ppermute(arr_next, shard_axis, [(d, d ^ h) for d in range(y1)]))  45.9 us
    ppermute x15, starting transfers between devices, prepare_orders(): made.append(ppermute(arr_next, shard_axis, [(d, d ^ h) for d in range(y1)]))  8.94 us
    unnamed x55, local copies, waits for them, and re-layouts  6.61 us
  transfers between devices with their start and end apart: 16, of which 12 were waited for; matrix products, arithmetic and copies ran while one was open for 2% of the time, Pallas kernels for 0%

profile of v1, /device:TPU:1, one launch (start us, length us, event | category | flops | bytes accessed | tf_op | source)
XLA Modules:
  0.0 267.7 jit_solution(10935259360231061925)
XLA Ops:
  10.4 2.2 convert_reduce_fusion.1
  12.6 1.5 multiply_subtract_fusion
  15.5 86.6 %all-reduce.2 = bf16[2,2,16,12288]{3,1,2,0:T(2,128)(2,1)} all-reduce(f32[2,2,16,12288]{3,1,2,0:T(2,128)S(1)} %pad_maximum_fusion), channel_id=3, replica_groups=mesh['lat'=16,'kpt'=16] {'lat'}, use_global_device_ids=true, to_apply=%region_0.0.clone | all-reduce | flops 786432 | bytes 4718592
  102.7 1.6 dynamic-slice_convert_fusion
  107.4 6.0 %collective-permute-start.11 = (bf16[2,2,1,768]{3,1,0,2:T(2,128)(2,1)S(1)}, bf16[2,2,1,768]{3,1,0,2:T(2,128)(2,1)S(1)}, u32[]{:S(2)}, u32[]{:S(2)}) collective-permute-start(bf16[2,2,1,768]{3,1,0,2:T(2,128)(2,1)S(1)} %get-tuple-element.20), channel_id=1, source_target_pairs={{0,192},{16,208},{32,224},{48,240},{64,128},{80,144},{96,160},{112... | collective-permute-start | bytes 18440 | tf_op jit(solution)/shard_map/ppermute | solution.py:31
  113.4 2.4 collective-permute-done
  115.8 4.0 %collective-permute-done.1 = bf16[2,2,1,768]{3,1,0,2:T(2,128)(2,1)S(1)} collective-permute-done((bf16[2,2,1,768]{3,1,0,2:T(2,128)(2,1)S(1)}, bf16[2,2,1,768]{3,1,0,2:T(2,128)(2,1)S(1)}, u32[]{:S(2)}, u32[]{:S(2)}) %collective-permute-start.1) | collective-permute-done | bytes 6176 | tf_op jit(solution)/shard_map/ppermute | solution.py:31
  119.8 3.7 %collective-permute-done.2 = bf16[2,2,1,768]{3,1,0,2:T(2,128)(2,1)S(1)} collective-permute-done((bf16[2,2,1,768]{3,1,0,2:T(2,128)(2,1)S(1)}, bf16[2,2,1,768]{3,1,0,2:T(2,128)(2,1)S(1)}, u32[]{:S(2)}, u32[]{:S(2)}) %collective-permute-start.2) | collective-permute-done | bytes 6176 | tf_op jit(solution)/shard_map/ppermute | solution.py:31
  123.5 2.8 %collective-permute-done.3 = bf16[2,2,1,768]{3,1,0,2:T(2,128)(2,1)S(1)} collective-permute-done((bf16[2,2,1,768]{3,1,0,2:T(2,128)(2,1)S(1)}, bf16[2,2,1,768]{3,1,0,2:T(2,128)(2,1)S(1)}, u32[]{:S(2)}, u32[]{:S(2)}) %collective-permute-start.3) | collective-permute-done | bytes 6176 | tf_op jit(solution)/shard_map/ppermute | solution.py:31
  126.3 3.4 %collective-permute-done.4 = bf16[2,2,1,768]{3,1,0,2:T(2,128)(2,1)S(1)} collective-permute-done((bf16[2,2,1,768]{3,1,0,2:T(2,128)(2,1)S(1)}, bf16[2,2,1,768]{3,1,0,2:T(2,128)(2,1)S(1)}, u32[]{:S(2)}, u32[]{:S(2)}) %collective-permute-start.4) | collective-permute-done | bytes 6176 | tf_op jit(solution)/shard_map/ppermute | solution.py:31
  129.7 4.9 %collective-permute-done.5 = bf16[2,2,1,768]{3,1,0,2:T(2,128)(2,1)S(1)} collective-permute-done((bf16[2,2,1,768]{3,1,0,2:T(2,128)(2,1)S(1)}, bf16[2,2,1,768]{3,1,0,2:T(2,128)(2,1)S(1)}, u32[]{:S(2)}, u32[]{:S(2)}) %collective-permute-start.5) | collective-permute-done | bytes 6176 | tf_op jit(solution)/shard_map/ppermute | solution.py:31
  134.5 4.6 %collective-permute-done.6 = bf16[2,2,1,768]{3,1,0,2:T(2,128)(2,1)S(1)} collective-permute-done((bf16[2,2,1,768]{3,1,0,2:T(2,128)(2,1)S(1)}, bf16[2,2,1,768]{3,1,0,2:T(2,128)(2,1)S(1)}, u32[]{:S(2)}, u32[]{:S(2)}) %collective-permute-start.6) | collective-permute-done | bytes 6176 | tf_op jit(solution)/shard_map/ppermute | solution.py:31
  139.1 4.0 %collective-permute-done.7 = bf16[2,2,1,768]{3,1,0,2:T(2,128)(2,1)S(1)} collective-permute-done((bf16[2,2,1,768]{3,1,0,2:T(2,128)(2,1)S(1)}, bf16[2,2,1,768]{3,1,0,2:T(2,128)(2,1)S(1)}, u32[]{:S(2)}, u32[]{:S(2)}) %collective-permute-start.7) | collective-permute-done | bytes 6176 | tf_op jit(solution)/shard_map/ppermute | solution.py:31
  143.1 4.9 %collective-permute-done.8 = bf16[2,2,1,768]{3,1,0,2:T(2,128)(2,1)S(1)} collective-permute-done((bf16[2,2,1,768]{3,1,0,2:T(2,128)(2,1)S(1)}, bf16[2,2,1,768]{3,1,0,2:T(2,128)(2,1)S(1)}, u32[]{:S(2)}, u32[]{:S(2)}) %collective-permute-start.8) | collective-permute-done | bytes 6176 | tf_op jit(solution)/shard_map/ppermute | solution.py:31
  148.0 6.4 %collective-permute-done.9 = bf16[2,2,1,768]{3,1,0,2:T(2,128)(2,1)S(1)} collective-permute-done((bf16[2,2,1,768]{3,1,0,2:T(2,128)(2,1)S(1)}, bf16[2,2,1,768]{3,1,0,2:T(2,128)(2,1)S(1)}, u32[]{:S(2)}, u32[]{:S(2)}) %collective-permute-start.9) | collective-permute-done | bytes 6176 | tf_op jit(solution)/shard_map/ppermute | solution.py:31
  155.5 5.0 %collective-permute-done.10 = bf16[2,2,1,768]{3,1,0,2:T(2,128)(2,1)S(1)} collective-permute-done((bf16[2,2,1,768]{3,1,0,2:T(2,128)(2,1)S(1)}, bf16[2,2,1,768]{3,1,0,2:T(2,128)(2,1)S(1)}, u32[]{:S(2)}, u32[]{:S(2)}) %collective-permute-start.10) | collective-permute-done | bytes 6176 | tf_op jit(solution)/shard_map/ppermute | solution.py:31
  163.4 1.5 copy.119
  164.9 1.5 copy.118
  167.2 57.7 %all-gather.3.cloned.1.call-done = bf16[2,2,256,1,768]{4,2,1,3,0:T(8,128)(2,1)} async-done(((bf16[2,2,16,1,768]{4,2,1,3,0:T(8,128)(2,1)}), bf16[2,2,256,1,768]{4,2,1,3,0:T(8,128)(2,1)}) %all-gather.3.cloned.1.call-update) | async-done | bytes 1572880 | tf_op jit(solution)/shard_map/all_gather | solution.py:106
  224.9 1.7 fusion.9
  226.6 1.6 fusion.1
  230.4 1.5 copy.87
  232.0 2.2 copy.90
  234.1 1.5 fusion.21
  238.2 2.3 fusion.10
  241.2 2.3 fusion.14
  243.5 2.3 fusion.12
  245.7 3.5 %copy.102 = f32[64,2,3,16,16]{0,3,4,2,1:T(8,128)} copy(f32[64,2,3,16,16]{4,3,2,1,0:T(8,128)} %fusion.10) | data formatting | bytes 786432 | tf_op jit(solution)/shard_map/qkac,kqman->kqmcn/dot_general | solution.py:132
  249.2 2.3 copy.97
  251.5 3.7 %copy.101 = f32[64,2,3,16,16]{0,3,4,2,1:T(8,128)} copy(f32[64,2,3,16,16]{4,3,2,1,0:T(8,128)} %fusion.14) | data formatting | bytes 786432 | tf_op jit(solution)/shard_map/qkac,kqman->kqmcn/dot_general | solution.py:130
  255.2 2.3 copy.98
  257.5 2.1 fusion.7
  (110 shorter events, 19.4 us)
Async XLA Ops:
  6.5 218.4 %all-gather.3.cloned.1.call-start = ((), (), s32[]{:S(2)}) async-start(), calls=%async_computation | async-start | bytes 1671168 | tf_op jit(solution)/shard_map/all_gather | solution.py:106
  9.7 0.7 copy-start.10
  15.5 86.6 %copy-start.15 = (u32[256]{0:T(256)S(1)}, u32[256]{0:T(256)}, u32[]{:S(2)}) copy-start(u32[256]{0:T(256)} %constant.53) | copy-start | bytes 3076
  15.5 88.9 %copy-start.7 = (bf16[2,2,48,48]{3,2,1,0:T(8,128)(2,1)S(1)}, bf16[2,2,48,48]{3,2,1,0:T(8,128)(2,1)}, u32[]{:S(2)}) copy-start(bf16[2,2,48,48]{3,2,1,0:T(8,128)(2,1)} %param.19) | copy-start | bytes 55300
  102.1 60.0 %copy-start.12 = (s32[256,3]{0,1:T(4,128)S(1)}, s32[256,3]{0,1:T(4,128)}, u32[]{:S(2)}) copy-start(s32[256,3]{0,1:T(4,128)} %param.15) | copy-start | bytes 9220
  102.1 60.0 %copy-start.11 = (s32[64,16]{0,1:T(8,128)S(1)}, s32[64,16]{0,1:T(8,128)}, u32[]{:S(2)}) copy-start(s32[64,16]{0,1:T(8,128)} %param.22) | copy-start | bytes 12292
  102.1 60.0 %copy-start.8 = (bf16[2,64,16,16]{1,3,2,0:T(8,128)(2,1)S(1)}, bf16[2,64,16,16]{1,3,2,0:T(8,128)(2,1)}, u32[]{:S(2)}) copy-start(bf16[2,64,16,16]{1,3,2,0:T(8,128)(2,1)} %param.20) | copy-start | bytes 196612
  104.4 59.0 %copy-start.6 = (bf16[2,2,64,16,16]{2,4,3,1,0:T(8,128)(2,1)S(1)}, bf16[2,2,64,16,16]{2,4,3,1,0:T(8,128)(2,1)}, u32[]{:S(2)}) copy-start(bf16[2,2,64,16,16]{2,4,3,1,0:T(8,128)(2,1)} %param.21) | copy-start | bytes 393220
  105.5 55.1 %collective-permute-start.14 = (bf16[2,2,1,768]{3,1,0,2:T(2,128)(2,1)S(1)}, bf16[2,2,1,768]{3,1,0,2:T(2,128)(2,1)S(1)}, u32[]{:S(2)}, u32[]{:S(2)}) collective-permute-start(bf16[2,2,1,768]{3,1,0,2:T(2,128)(2,1)S(1)} %get-tuple-element.17), channel_id=1, source_target_pairs={{0,240},{16,224},{32,208},{48,192},{64,176},{80,160},{96,144},{112... | collective-permute-start | bytes 18440 | tf_op jit(solution)/shard_map/ppermute | solution.py:31
  106.7 53.9 %collective-permute-start.13 = (bf16[2,2,1,768]{3,1,0,2:T(2,128)(2,1)S(1)}, bf16[2,2,1,768]{3,1,0,2:T(2,128)(2,1)S(1)}, u32[]{:S(2)}, u32[]{:S(2)}) collective-permute-start(bf16[2,2,1,768]{3,1,0,2:T(2,128)(2,1)S(1)} %get-tuple-element.18), channel_id=1, source_target_pairs={{0,224},{16,240},{32,192},{48,208},{64,160},{80,176},{96,128},{112... | collective-permute-start | bytes 18440 | tf_op jit(solution)/shard_map/ppermute | solution.py:31
  107.4 53.1 %collective-permute-start.12 = (bf16[2,2,1,768]{3,1,0,2:T(2,128)(2,1)S(1)}, bf16[2,2,1,768]{3,1,0,2:T(2,128)(2,1)S(1)}, u32[]{:S(2)}, u32[]{:S(2)}) collective-permute-start(bf16[2,2,1,768]{3,1,0,2:T(2,128)(2,1)S(1)} %get-tuple-element.19), channel_id=1, source_target_pairs={{0,208},{16,192},{32,240},{48,224},{64,144},{80,128},{96,176},{112... | collective-permute-start | bytes 18440 | tf_op jit(solution)/shard_map/ppermute | solution.py:31
  107.4 53.1 %collective-permute-start.11 = (bf16[2,2,1,768]{3,1,0,2:T(2,128)(2,1)S(1)}, bf16[2,2,1,768]{3,1,0,2:T(2,128)(2,1)S(1)}, u32[]{:S(2)}, u32[]{:S(2)}) collective-permute-start(bf16[2,2,1,768]{3,1,0,2:T(2,128)(2,1)S(1)} %get-tuple-element.20), channel_id=1, source_target_pairs={{0,192},{16,208},{32,224},{48,240},{64,128},{80,144},{96,160},{112... | collective-permute-start | bytes 18440 | tf_op jit(solution)/shard_map/ppermute | solution.py:31
  113.3 2.5 collective-permute-start
  115.8 4.0 %collective-permute-start.1 = (bf16[2,2,1,768]{3,1,0,2:T(2,128)(2,1)S(1)}, bf16[2,2,1,768]{3,1,0,2:T(2,128)(2,1)S(1)}, u32[]{:S(2)}, u32[]{:S(2)}) collective-permute-start(bf16[2,2,1,768]{3,1,0,2:T(2,128)(2,1)S(1)} %get-tuple-element.30), channel_id=1, source_target_pairs={{0,32},{16,48},{32,0},{48,16},{64,96},{80,112},{96,64},{112,80},{1... | collective-permute-start | bytes 18440 | tf_op jit(solution)/shard_map/ppermute | solution.py:31
  119.8 3.7 %collective-permute-start.2 = (bf16[2,2,1,768]{3,1,0,2:T(2,128)(2,1)S(1)}, bf16[2,2,1,768]{3,1,0,2:T(2,128)(2,1)S(1)}, u32[]{:S(2)}, u32[]{:S(2)}) collective-permute-start(bf16[2,2,1,768]{3,1,0,2:T(2,128)(2,1)S(1)} %get-tuple-element.29), channel_id=1, source_target_pairs={{0,48},{16,32},{32,16},{48,0},{64,112},{80,96},{96,80},{112,64},{1... | collective-permute-start | bytes 18440 | tf_op jit(solution)/shard_map/ppermute | solution.py:31
  123.5 2.8 %collective-permute-start.3 = (bf16[2,2,1,768]{3,1,0,2:T(2,128)(2,1)S(1)}, bf16[2,2,1,768]{3,1,0,2:T(2,128)(2,1)S(1)}, u32[]{:S(2)}, u32[]{:S(2)}) collective-permute-start(bf16[2,2,1,768]{3,1,0,2:T(2,128)(2,1)S(1)} %get-tuple-element.28), channel_id=1, source_target_pairs={{0,64},{16,80},{32,96},{48,112},{64,0},{80,16},{96,32},{112,48},{1... | collective-permute-start | bytes 18440 | tf_op jit(solution)/shard_map/ppermute | solution.py:31
  126.3 3.4 %collective-permute-start.4 = (bf16[2,2,1,768]{3,1,0,2:T(2,128)(2,1)S(1)}, bf16[2,2,1,768]{3,1,0,2:T(2,128)(2,1)S(1)}, u32[]{:S(2)}, u32[]{:S(2)}) collective-permute-start(bf16[2,2,1,768]{3,1,0,2:T(2,128)(2,1)S(1)} %get-tuple-element.27), channel_id=1, source_target_pairs={{0,80},{16,64},{32,112},{48,96},{64,16},{80,0},{96,48},{112,32},{1... | collective-permute-start | bytes 18440 | tf_op jit(solution)/shard_map/ppermute | solution.py:31
  129.6 4.9 %collective-permute-start.5 = (bf16[2,2,1,768]{3,1,0,2:T(2,128)(2,1)S(1)}, bf16[2,2,1,768]{3,1,0,2:T(2,128)(2,1)S(1)}, u32[]{:S(2)}, u32[]{:S(2)}) collective-permute-start(bf16[2,2,1,768]{3,1,0,2:T(2,128)(2,1)S(1)} %get-tuple-element.26), channel_id=1, source_target_pairs={{0,96},{16,112},{32,64},{48,80},{64,32},{80,48},{96,0},{112,16},{1... | collective-permute-start | bytes 18440 | tf_op jit(solution)/shard_map/ppermute | solution.py:31
  134.5 4.6 %collective-permute-start.6 = (bf16[2,2,1,768]{3,1,0,2:T(2,128)(2,1)S(1)}, bf16[2,2,1,768]{3,1,0,2:T(2,128)(2,1)S(1)}, u32[]{:S(2)}, u32[]{:S(2)}) collective-permute-start(bf16[2,2,1,768]{3,1,0,2:T(2,128)(2,1)S(1)} %get-tuple-element.25), channel_id=1, source_target_pairs={{0,112},{16,96},{32,80},{48,64},{64,48},{80,32},{96,16},{112,0},{1... | collective-permute-start | bytes 18440 | tf_op jit(solution)/shard_map/ppermute | solution.py:31
  139.1 4.0 %collective-permute-start.7 = (bf16[2,2,1,768]{3,1,0,2:T(2,128)(2,1)S(1)}, bf16[2,2,1,768]{3,1,0,2:T(2,128)(2,1)S(1)}, u32[]{:S(2)}, u32[]{:S(2)}) collective-permute-start(bf16[2,2,1,768]{3,1,0,2:T(2,128)(2,1)S(1)} %get-tuple-element.24), channel_id=1, source_target_pairs={{0,128},{16,144},{32,160},{48,176},{64,192},{80,208},{96,224},{112... | collective-permute-start | bytes 18440 | tf_op jit(solution)/shard_map/ppermute | solution.py:31
  143.1 4.9 %collective-permute-start.8 = (bf16[2,2,1,768]{3,1,0,2:T(2,128)(2,1)S(1)}, bf16[2,2,1,768]{3,1,0,2:T(2,128)(2,1)S(1)}, u32[]{:S(2)}, u32[]{:S(2)}) collective-permute-start(bf16[2,2,1,768]{3,1,0,2:T(2,128)(2,1)S(1)} %get-tuple-element.23), channel_id=1, source_target_pairs={{0,144},{16,128},{32,176},{48,160},{64,208},{80,192},{96,240},{112... | collective-permute-start | bytes 18440 | tf_op jit(solution)/shard_map/ppermute | solution.py:31
  148.0 6.4 %collective-permute-start.9 = (bf16[2,2,1,768]{3,1,0,2:T(2,128)(2,1)S(1)}, bf16[2,2,1,768]{3,1,0,2:T(2,128)(2,1)S(1)}, u32[]{:S(2)}, u32[]{:S(2)}) collective-permute-start(bf16[2,2,1,768]{3,1,0,2:T(2,128)(2,1)S(1)} %get-tuple-element.22), channel_id=1, source_target_pairs={{0,160},{16,176},{32,128},{48,144},{64,224},{80,240},{96,192},{112... | collective-permute-start | bytes 18440 | tf_op jit(solution)/shard_map/ppermute | solution.py:31
  154.4 6.1 %collective-permute-start.10 = (bf16[2,2,1,768]{3,1,0,2:T(2,128)(2,1)S(1)}, bf16[2,2,1,768]{3,1,0,2:T(2,128)(2,1)S(1)}, u32[]{:S(2)}, u32[]{:S(2)}) collective-permute-start(bf16[2,2,1,768]{3,1,0,2:T(2,128)(2,1)S(1)} %get-tuple-element.21), channel_id=1, source_target_pairs={{0,176},{16,160},{32,144},{48,128},{64,240},{80,224},{96,208},{112... | collective-permute-start | bytes 18440 | tf_op jit(solution)/shard_map/ppermute | solution.py:31
  161.4 5.1 %copy-start.14 = (s32[256]{0:T(256)S(1)}, s32[256]{0:T(256)}, u32[]{:S(2)}) copy-start(s32[256]{0:T(256)} %param.16) | copy-start | bytes 3076
  161.4 5.1 %copy-start.13 = (f32[64,3]{0,1:T(4,128)S(1)}, f32[64,3]{0,1:T(4,128)}, u32[]{:S(2)}) copy-start(f32[64,3]{0,1:T(4,128)} %param.18) | copy-start | bytes 2308
  161.4 5.1 %copy-start.9 = (s32[2,64,16]{1,2,0:T(8,128)S(1)}, s32[2,64,16]{1,2,0:T(8,128)}, u32[]{:S(2)}) copy-start(s32[2,64,16]{1,2,0:T(8,128)} %param.23) | copy-start | bytes 24580
  224.9 4.3 %copy-start.1 = (bf16[2,2,256,1,768]{4,2,1,3,0:T(8,128)(2,1)S(1)}, bf16[2,2,256,1,768]{4,2,1,3,0:T(8,128)(2,1)}, u32[]{:S(2)}) copy-start(bf16[2,2,256,1,768]{4,2,1,3,0:T(8,128)(2,1)} %all-gather.3.cloned.1.call-done) | copy-start | bytes 4718596
  236.2 1.0 copy-start.4
  237.1 1.0 copy-start.2
  238.2 2.3 copy-start.3
  251.5 3.7 %copy-start = (f32[64,2,3,16,16]{4,3,2,1,0:T(8,128)S(1)}, f32[64,2,3,16,16]{4,3,2,1,0:T(8,128)}, u32[]{:S(2)}) copy-start(f32[64,2,3,16,16]{4,3,2,1,0:T(8,128)} %fusion.12) | copy-start | bytes 1179652
  255.2 2.3 copy-start.5
Sparse Core Ops, SparseCore 0:
  162.2 62.6 all-gather.2
